TPU v7x, 512 devices: a whole 4x8x8 slice. The times are simulated.
512 devices in a mesh: seq: 32 (over x, z), exp: 16 (over y, core).
Axes of the slice: x: 4, y: 8, z: 8, core: 2. Of those that a mesh axis runs over, the one named last changes fastest.
Arguments:
- queries: bfloat16 [8192, 2048], P('seq', 'exp'), may hold values from -112 to 112
- key_rows: bfloat16 [8192, 2048], P('seq', 'exp'), may hold values from -4 to 4
- value_rows: bfloat16 [8192, 2048], P('seq', 'exp'), may hold values from -6 to 6
- out_grad: bfloat16 [8192, 2048], P('seq', 'exp'), may hold values from -6 to 6
- expert_ids: int32 [8192, 2], P('seq'), may hold values from 0 to 31, all different within a row
- gate_values: float32 [8192, 2], P('seq'), may hold values from 0.1 to 1
- alibi_slope: float32 [16], P('exp'), may hold values from 0.00012207031 to 0.1
- expert_in: bfloat16 [32, 2048, 4096], P('seq', None, 'exp'), may hold values from -0.125 to 0.125
- expert_out: bfloat16 [32, 4096, 2048], P('seq', 'exp'), may hold values from -0.09375 to 0.09375
Outputs:
- query_grad: bfloat16 [8192, 2048], P('seq', 'exp')
- key_grad: bfloat16 [8192, 2048], P('seq', 'exp')
- value_grad: bfloat16 [8192, 2048], P('seq', 'exp')
- expert_in_grad: bfloat16 [32, 2048, 4096], P('seq', None, 'exp')
- expert_out_grad: bfloat16 [32, 4096, 2048], P('seq', 'exp')
Inputs may be any that keep to these rules, and one draw needn't show every extreme that they name: `expert_ids`: each token names two different experts.
All inputs are finite; a program needn't handle non-finite values.
Results may differ from a plain program's by a relative error of at most 0.024.
Values may be sent and summed in bfloat16 or wider, within the bound.
A program may use at most 128 MiB of HBM per device.

v0:
```python
import jax
import jax.numpy as jnp
from jax import lax
from jax.sharding import PartitionSpec as P

HD = 128
WCH = 16


def shifted(block, axis, distance):
    devices = range(lax.axis_size(axis))
    route = [(i - distance, i) for i in devices if i - distance in devices]
    return lax.ppermute(block, axis, route)


def window_scores(query_heads, key_stack, slopes, seq_index, window):
    score_scale = HD ** (-0.5)
    block_len = query_heads.shape[0]
    raw_scores = (
        jnp.einsum("ihd,jhd->hij", query_heads, key_stack, preferred_element_type=jnp.float32)
        * score_scale
    )
    row_pos = lax.broadcasted_iota(jnp.int32, (block_len, key_stack.shape[0]), 0)
    col_pos = lax.broadcasted_iota(jnp.int32, (block_len, key_stack.shape[0]), 1)
    back_block = col_pos // block_len
    distance = row_pos - col_pos % block_len + back_block * block_len
    in_window = (distance >= 0) & (distance < window) & (seq_index - back_block >= 0)
    biased = raw_scores - slopes[:, None, None] * distance.astype(jnp.float32)[None]
    return jnp.where(in_window[None], biased, -jnp.inf)


def slot_routing(expert_ids, experts, capacity):
    flat_ids = jnp.concatenate([expert_ids[:, 0], expert_ids[:, 1]])
    entry_count = flat_ids.shape[0]
    expert_cols = lax.broadcasted_iota(jnp.int32, (entry_count, experts), 1)
    one_hot = (flat_ids[:, None] == expert_cols).astype(jnp.int32)
    before = jnp.cumsum(one_hot, axis=0) - one_hot
    position = jnp.sum(before * one_hot, axis=1)
    is_kept = position < capacity
    slot_index = flat_ids * capacity + position
    slot_rows = lax.broadcasted_iota(jnp.int32, (experts * capacity, entry_count), 0)
    return ((slot_rows == slot_index[None, :]) & is_kept[None, :]).astype(jnp.bfloat16)


def per_device(
    queries,
    key_rows,
    value_rows,
    out_grad,
    expert_ids,
    gate_values,
    alibi_slope,
    expert_in,
    expert_out,
):
    score_scale = HD ** (-0.5)
    block_len = queries.shape[0]
    features = queries.shape[1]
    head_count = features // HD
    seq_index = lax.axis_index("seq")
    stretches = WCH + 1
    window = WCH * block_len

    def relay_keys(step, carry):
        stack_keys, stack_values, current_keys, current_values = carry
        current_keys, current_values = shifted((current_keys, current_values), "seq", 1)
        stack_keys = lax.dynamic_update_index_in_dim(stack_keys, current_keys, step, 0)
        stack_values = lax.dynamic_update_index_in_dim(stack_values, current_values, step, 0)
        return (stack_keys, stack_values, current_keys, current_values)

    empty_stack = jnp.zeros((stretches, block_len, features), jnp.bfloat16)
    start_keys = lax.dynamic_update_index_in_dim(empty_stack, key_rows, 0, 0)
    start_values = lax.dynamic_update_index_in_dim(empty_stack, value_rows, 0, 0)
    key_stack, value_stack, unused_keys, unused_values = lax.fori_loop(
        1, stretches, relay_keys, (start_keys, start_values, key_rows, value_rows)
    )
    key_block = key_stack.reshape(stretches * block_len, head_count, HD)
    value_block = value_stack.reshape(stretches * block_len, head_count, HD)
    query_heads = queries.reshape(block_len, head_count, HD)
    scores = window_scores(query_heads, key_block, alibi_slope, seq_index, window)
    log_norm = jax.nn.logsumexp(scores, axis=2)
    probs_full = jnp.exp(scores - log_norm[:, :, None])
    weights = probs_full.astype(jnp.bfloat16)
    attn_heads = jnp.einsum(
        "hij,jhd->ihd", weights, value_block, preferred_element_type=jnp.float32
    ).astype(jnp.bfloat16)
    attn_out = attn_heads.reshape(block_len, features)
    experts = lax.axis_size("seq")
    capacity = 5 * block_len // (2 * experts)
    routing = slot_routing(expert_ids, experts, capacity)
    both_tokens = jnp.concatenate([attn_out, attn_out])
    scaled_grad = jnp.concatenate(
        [gate_values[:, 0:1] * out_grad, gate_values[:, 1:2] * out_grad]
    ).astype(jnp.bfloat16)
    send_tokens = jnp.dot(routing, both_tokens, preferred_element_type=jnp.float32).astype(
        jnp.bfloat16
    )
    send_grads = jnp.dot(routing, scaled_grad, preferred_element_type=jnp.float32).astype(
        jnp.bfloat16
    )
    recv_tokens, recv_grads = (
        lax.all_to_all(send_tokens, "seq", split_axis=0, concat_axis=0, tiled=True),
        lax.all_to_all(send_grads, "seq", split_axis=0, concat_axis=0, tiled=True),
    )
    weight_in = expert_in[0]
    weight_out = expert_out[0]
    full_tokens = lax.all_gather(recv_tokens, "exp", axis=1, tiled=True)
    pre_act = jnp.dot(full_tokens, weight_in, preferred_element_type=jnp.float32)
    full_grads = lax.all_gather(recv_grads, "exp", axis=1, tiled=True)
    logistic = jax.nn.sigmoid(pre_act)
    hidden = (pre_act * logistic).astype(jnp.bfloat16)
    through_out = lax.dot_general(
        full_grads, weight_out, (((1,), (1,)), ((), ())), preferred_element_type=jnp.float32
    )
    hidden_grad = (through_out * logistic * (1.0 + pre_act * (1.0 - logistic))).astype(jnp.bfloat16)
    out_weight_grad = lax.dot_general(
        hidden, full_grads, (((0,), (0,)), ((), ())), preferred_element_type=jnp.float32
    ).astype(jnp.bfloat16)
    in_weight_grad = lax.dot_general(
        full_tokens, hidden_grad, (((0,), (0,)), ((), ())), preferred_element_type=jnp.float32
    ).astype(jnp.bfloat16)
    back_rows = lax.psum_scatter(
        lax.dot_general(
            weight_in, hidden_grad, (((1,), (1,)), ((), ())), preferred_element_type=jnp.float32
        ).astype(jnp.bfloat16),
        "exp",
        scatter_dimension=0,
        tiled=True,
    )
    returned = lax.all_to_all(back_rows, "seq", split_axis=1, concat_axis=1, tiled=True)
    combined = lax.dot_general(
        routing, returned, (((0,), (1,)), ((), ())), preferred_element_type=jnp.float32
    )
    attn_grad = (out_grad.astype(jnp.float32) + combined[:block_len] + combined[block_len:]).astype(
        jnp.bfloat16
    )
    grad_heads = attn_grad.reshape(block_len, head_count, HD)
    row_delta = jnp.einsum(
        "ihd,ihd->hi", grad_heads, attn_heads, preferred_element_type=jnp.float32
    )
    dprob = jnp.einsum("ihd,jhd->hij", grad_heads, value_block, preferred_element_type=jnp.float32)
    dscore = (probs_full * (dprob - row_delta[:, :, None])).astype(jnp.bfloat16)
    query_grad = (
        jnp.einsum("hij,jhd->ihd", dscore, key_block, preferred_element_type=jnp.float32)
        * score_scale
    ).astype(jnp.bfloat16)
    key_parts = (
        jnp.einsum("hij,ihd->jhd", dscore, query_heads, preferred_element_type=jnp.float32)
        * score_scale
    ).reshape(stretches, block_len, features)
    value_parts = jnp.einsum(
        "hij,ihd->jhd", weights, grad_heads, preferred_element_type=jnp.float32
    ).reshape(stretches, block_len, features)

    def relay_grads(step, carry):
        key_acc, value_acc = carry
        key_acc, value_acc = (
            shifted(key_acc.astype(jnp.bfloat16), "seq", -1).astype(key_acc.dtype),
            shifted(value_acc.astype(jnp.bfloat16), "seq", -1).astype(value_acc.dtype),
        )
        index = stretches - 1 - step
        key_acc = key_acc + lax.dynamic_index_in_dim(key_parts, index, 0, keepdims=False)
        value_acc = value_acc + lax.dynamic_index_in_dim(value_parts, index, 0, keepdims=False)
        return (key_acc, value_acc)

    key_total, value_total = lax.fori_loop(
        1, stretches, relay_grads, (key_parts[stretches - 1], value_parts[stretches - 1])
    )
    key_grad = key_total.astype(jnp.bfloat16)
    value_grad = value_total.astype(jnp.bfloat16)
    return (
        query_grad.reshape(block_len, features),
        key_grad,
        value_grad,
        in_weight_grad[None],
        out_weight_grad[None],
    )


def solution(mesh):
    return jax.shard_map(
        per_device,
        mesh=mesh,
        in_specs=(
            P("seq", "exp"),
            P("seq", "exp"),
            P("seq", "exp"),
            P("seq", "exp"),
            P("seq", None),
            P("seq", None),
            P("exp"),
            P("seq", None, "exp"),
            P("seq", "exp", None),
        ),
        out_specs=(
            P("seq", "exp"),
            P("seq", "exp"),
            P("seq", "exp"),
            P("seq", None, "exp"),
            P("seq", "exp", None),
        ),
        check_vma=False,
    )
```

profile of v0, /device:TPU:2, one launch (start us, length us, event | category | flops | bytes accessed | tf_op | source)
XLA Modules:
  0.0 586.6 jit_solution(2084339012505833438)
XLA Ops:
  14.8 170.1 %while.36 = (s32[]{:T(128)}, bf16[17,256,128]{2,1,0:T(8,128)(2,1)S(1)}, bf16[17,256,128]{2,1,0:T(8,128)(2,1)S(1)}, bf16[256,128]{1,0:T(8,128)(2,1)S(1)}, bf16[25...) while((s32[]{:T(128)}, bf16[17,256,128]{2,1,0:T(8,128)(2,1)S(1)}, ...), condition=%wide.region_1.2_spmd, body=%wide.region_0.1_spmd.sunk | while | flops 5 | bytes 1048783 | solution.py:74
  14.8 4.3 collective-permute-start.1
  19.1 4.3 collective-permute-start
  23.4 4.6 collective-permute-done.1
  35.1 3.7 collective-permute-done.1
  42.1 3.8 collective-permute-start
  52.4 4.0 collective-permute-start
  62.6 3.7 collective-permute-start
  85.1 4.4 collective-permute-done.1
  95.3 4.4 collective-permute-done.1
  106.2 5.0 collective-permute-done.1
  117.0 4.4 collective-permute-done.1
  127.3 5.0 collective-permute-done.1
  137.5 4.8 collective-permute-done.1
  147.8 4.4 collective-permute-done.1
  158.0 4.4 collective-permute-done.1
  168.3 4.4 collective-permute-done.1
  178.5 4.4 collective-permute-done.1
  184.9 5.8 fusion.71
  194.7 15.8 %all_to_all.36 = bf16[32,20,128]{2,1,0:T(8,128)(2,1)} all-to-all(bf16[32,20,128]{2,1,0:T(8,128)(2,1)S(1)} %all_to_all.27), channel_id=1, replica_groups=mesh['seq'=32,'exp'=16] {'seq'}, dimensions={0} | all-to-all | bytes 327680 | tf_op jit(solution)/shard_map/all_to_all | solution.py:102
  215.3 15.9 %all_to_all.37 = bf16[32,20,128]{2,1,0:T(8,128)(2,1)} all-to-all(bf16[32,20,128]{2,1,0:T(8,128)(2,1)S(1)} %all_to_all.24), channel_id=1, replica_groups=mesh['seq'=32,'exp'=16] {'seq'}, dimensions={0} | all-to-all | bytes 327680 | tf_op jit(solution)/shard_map/all_to_all | solution.py:103
  232.9 22.8 %all-gather.5.cloned.1.call-done = bf16[640,2048]{1,0:T(8,128)(2,1)} async-done(((bf16[640,128]{1,0:T(8,128)(2,1)}), bf16[640,2048]{1,0:T(8,128)(2,1)}) %all-gather.5.cloned.1.call-update) | async-done | bytes 2621456 | tf_op jit(solution)/shard_map/all_gather | solution.py:107
  259.2 43.8 %all-gather.3.cloned.1.call-done = bf16[640,2048]{1,0:T(8,128)(2,1)} async-done(((bf16[640,128]{1,0:T(8,128)(2,1)}), bf16[640,2048]{1,0:T(8,128)(2,1)}) %all-gather.3.cloned.1.call-update) | async-done | bytes 2621456 | tf_op jit(solution)/shard_map/all_gather | solution.py:109
  309.2 4.4 copy.33
  313.6 4.0 fusion.14
  317.6 57.7 %reduce-scatter.4.cloned.1.call-done = bf16[128,640]{1,0:T(8,128)(2,1)} async-done(((bf16[2048,640]{1,0:T(8,128)(2,1)}), bf16[128,640]{1,0:T(8,128)(2,1)}) %reduce-scatter.4.cloned.1.call-update) | async-done | bytes 163856
  377.0 10.5 %all-to-all-start.2 = ((bf16[128,32,20]{0,2,1:T(8,128)(2,1)}), bf16[128,32,20]{0,2,1:T(8,128)(2,1)S(1)}, u32[]{:S(2)}, u32[]{:S(2)}) async-start(bf16[128,32,20]{0,2,1:T(8,128)(2,1)} %all_to_all.30), calls=%async_computation.2 | async-start | bytes 393216 | tf_op jit(solution)/shard_map/all_to_all | solution.py:130
  387.5 3.8 fusion.13
  391.3 5.7 all-to-all-done.2
  403.4 4.0 fusion.4
  412.9 166.5 %while.37 = (s32[]{:T(128)}, bf16[256,128]{1,0:T(8,128)(2,1)S(1)}, bf16[256,128]{1,0:T(8,128)(2,1)S(1)}, f32[17,256,128]{2,1,0:T(8,128)S(1)}, f32[17,256,128]{2,...) while((s32[]{:T(128)}, bf16[256,128]{1,0:T(8,128)(2,1)S(1)}, ...), condition=%wide.region_9.10_spmd, body=%wide.region_8.9_spmd.sunk | while | flops 196614 | bytes 1048803 | solution.py:166
  416.1 3.6 collective-permute-start.2
  422.3 5.7 collective-permute-start.3
  434.2 4.2 collective-permute-start.3
  444.6 4.0 collective-permute-start.3
  455.3 4.2 collective-permute-start.3
  465.7 4.0 collective-permute-start.3
  475.9 4.0 collective-permute-start.3
  486.2 4.0 collective-permute-start.3
  496.4 4.0 collective-permute-start.3
  506.6 4.0 collective-permute-start.3
  513.7 3.6 collective-permute-done.2
  517.3 3.6 collective-permute-start.3
  527.1 4.0 collective-permute-start.3
  537.3 4.6 collective-permute-start.3
  548.6 4.2 collective-permute-start.3
  559.0 4.0 collective-permute-start.3
  569.2 4.0 collective-permute-start.3
  (264 shorter events, 232.5 us)
Async XLA Ops:
  7.2 248.6 %all-gather.5.cloned.1.call-start = ((), (), s32[]{:S(2)}) async-start(), calls=%async_computation.5 | async-start | bytes 2785280 | tf_op jit(solution)/shard_map/all_gather | solution.py:107
  14.8 13.2 %collective-permute-start.1 = (bf16[256,128]{1,0:T(8,128)(2,1)S(1)}, bf16[256,128]{1,0:T(8,128)(2,1)S(1)}, u32[]{:S(2)}, u32[]{:S(2)}) collective-permute-start(bf16[256,128]{1,0:T(8,128)(2,1)S(1)} %get-tuple-element.375), channel_id=1, source_target_pairs={{0,16},{16,32},{32,48},{48,64},{64,80},{80,96},{96,112},{112,128},... | collective-permute-start | bytes 196616 | tf_op jit(solution)/shard_map/while/body/eval_jaxpr/ppermute | solution.py:13
  19.1 10.8 %collective-permute-start = (bf16[256,128]{1,0:T(8,128)(2,1)S(1)}, bf16[256,128]{1,0:T(8,128)(2,1)S(1)}, u32[]{:S(2)}, u32[]{:S(2)}) collective-permute-start(bf16[256,128]{1,0:T(8,128)(2,1)S(1)} %get-tuple-element.374), channel_id=1, source_target_pairs={{0,16},{16,32},{32,48},{48,64},{64,80},{80,96},{96,112},{112,128},... | collective-permute-start | bytes 196616 | tf_op jit(solution)/shard_map/while/body/eval_jaxpr/ppermute | solution.py:13
  30.0 8.9 %collective-permute-start.1 = (bf16[256,128]{1,0:T(8,128)(2,1)S(1)}, bf16[256,128]{1,0:T(8,128)(2,1)S(1)}, u32[]{:S(2)}, u32[]{:S(2)}) collective-permute-start(bf16[256,128]{1,0:T(8,128)(2,1)S(1)} %get-tuple-element.375), channel_id=1, source_target_pairs={{0,16},{16,32},{32,48},{48,64},{64,80},{80,96},{96,112},{112,128},... | collective-permute-start | bytes 196616 | tf_op jit(solution)/shard_map/while/body/eval_jaxpr/ppermute | solution.py:13
  31.9 8.3 %collective-permute-start = (bf16[256,128]{1,0:T(8,128)(2,1)S(1)}, bf16[256,128]{1,0:T(8,128)(2,1)S(1)}, u32[]{:S(2)}, u32[]{:S(2)}) collective-permute-start(bf16[256,128]{1,0:T(8,128)(2,1)S(1)} %get-tuple-element.374), channel_id=1, source_target_pairs={{0,16},{16,32},{32,48},{48,64},{64,80},{80,96},{96,112},{112,128},... | collective-permute-start | bytes 196616 | tf_op jit(solution)/shard_map/while/body/eval_jaxpr/ppermute | solution.py:13
  40.2 8.7 %collective-permute-start.1 = (bf16[256,128]{1,0:T(8,128)(2,1)S(1)}, bf16[256,128]{1,0:T(8,128)(2,1)S(1)}, u32[]{:S(2)}, u32[]{:S(2)}) collective-permute-start(bf16[256,128]{1,0:T(8,128)(2,1)S(1)} %get-tuple-element.375), channel_id=1, source_target_pairs={{0,16},{16,32},{32,48},{48,64},{64,80},{80,96},{96,112},{112,128},... | collective-permute-start | bytes 196616 | tf_op jit(solution)/shard_map/while/body/eval_jaxpr/ppermute | solution.py:13
  42.1 8.3 %collective-permute-start = (bf16[256,128]{1,0:T(8,128)(2,1)S(1)}, bf16[256,128]{1,0:T(8,128)(2,1)S(1)}, u32[]{:S(2)}, u32[]{:S(2)}) collective-permute-start(bf16[256,128]{1,0:T(8,128)(2,1)S(1)} %get-tuple-element.374), channel_id=1, source_target_pairs={{0,16},{16,32},{32,48},{48,64},{64,80},{80,96},{96,112},{112,128},... | collective-permute-start | bytes 196616 | tf_op jit(solution)/shard_map/while/body/eval_jaxpr/ppermute | solution.py:13
  50.5 8.3 %collective-permute-start.1 = (bf16[256,128]{1,0:T(8,128)(2,1)S(1)}, bf16[256,128]{1,0:T(8,128)(2,1)S(1)}, u32[]{:S(2)}, u32[]{:S(2)}) collective-permute-start(bf16[256,128]{1,0:T(8,128)(2,1)S(1)} %get-tuple-element.375), channel_id=1, source_target_pairs={{0,16},{16,32},{32,48},{48,64},{64,80},{80,96},{96,112},{112,128},... | collective-permute-start | bytes 196616 | tf_op jit(solution)/shard_map/while/body/eval_jaxpr/ppermute | solution.py:13
  52.4 8.3 %collective-permute-start = (bf16[256,128]{1,0:T(8,128)(2,1)S(1)}, bf16[256,128]{1,0:T(8,128)(2,1)S(1)}, u32[]{:S(2)}, u32[]{:S(2)}) collective-permute-start(bf16[256,128]{1,0:T(8,128)(2,1)S(1)} %get-tuple-element.374), channel_id=1, source_target_pairs={{0,16},{16,32},{32,48},{48,64},{64,80},{80,96},{96,112},{112,128},... | collective-permute-start | bytes 196616 | tf_op jit(solution)/shard_map/while/body/eval_jaxpr/ppermute | solution.py:13
  60.7 8.3 %collective-permute-start.1 = (bf16[256,128]{1,0:T(8,128)(2,1)S(1)}, bf16[256,128]{1,0:T(8,128)(2,1)S(1)}, u32[]{:S(2)}, u32[]{:S(2)}) collective-permute-start(bf16[256,128]{1,0:T(8,128)(2,1)S(1)} %get-tuple-element.375), channel_id=1, source_target_pairs={{0,16},{16,32},{32,48},{48,64},{64,80},{80,96},{96,112},{112,128},... | collective-permute-start | bytes 196616 | tf_op jit(solution)/shard_map/while/body/eval_jaxpr/ppermute | solution.py:13
  62.6 8.3 %collective-permute-start = (bf16[256,128]{1,0:T(8,128)(2,1)S(1)}, bf16[256,128]{1,0:T(8,128)(2,1)S(1)}, u32[]{:S(2)}, u32[]{:S(2)}) collective-permute-start(bf16[256,128]{1,0:T(8,128)(2,1)S(1)} %get-tuple-element.374), channel_id=1, source_target_pairs={{0,16},{16,32},{32,48},{48,64},{64,80},{80,96},{96,112},{112,128},... | collective-permute-start | bytes 196616 | tf_op jit(solution)/shard_map/while/body/eval_jaxpr/ppermute | solution.py:13
  71.0 8.3 %collective-permute-start.1 = (bf16[256,128]{1,0:T(8,128)(2,1)S(1)}, bf16[256,128]{1,0:T(8,128)(2,1)S(1)}, u32[]{:S(2)}, u32[]{:S(2)}) collective-permute-start(bf16[256,128]{1,0:T(8,128)(2,1)S(1)} %get-tuple-element.375), channel_id=1, source_target_pairs={{0,16},{16,32},{32,48},{48,64},{64,80},{80,96},{96,112},{112,128},... | collective-permute-start | bytes 196616 | tf_op jit(solution)/shard_map/while/body/eval_jaxpr/ppermute | solution.py:13
  72.9 8.3 %collective-permute-start = (bf16[256,128]{1,0:T(8,128)(2,1)S(1)}, bf16[256,128]{1,0:T(8,128)(2,1)S(1)}, u32[]{:S(2)}, u32[]{:S(2)}) collective-permute-start(bf16[256,128]{1,0:T(8,128)(2,1)S(1)} %get-tuple-element.374), channel_id=1, source_target_pairs={{0,16},{16,32},{32,48},{48,64},{64,80},{80,96},{96,112},{112,128},... | collective-permute-start | bytes 196616 | tf_op jit(solution)/shard_map/while/body/eval_jaxpr/ppermute | solution.py:13
  81.2 8.3 %collective-permute-start.1 = (bf16[256,128]{1,0:T(8,128)(2,1)S(1)}, bf16[256,128]{1,0:T(8,128)(2,1)S(1)}, u32[]{:S(2)}, u32[]{:S(2)}) collective-permute-start(bf16[256,128]{1,0:T(8,128)(2,1)S(1)} %get-tuple-element.375), channel_id=1, source_target_pairs={{0,16},{16,32},{32,48},{48,64},{64,80},{80,96},{96,112},{112,128},... | collective-permute-start | bytes 196616 | tf_op jit(solution)/shard_map/while/body/eval_jaxpr/ppermute | solution.py:13
  83.1 8.3 %collective-permute-start = (bf16[256,128]{1,0:T(8,128)(2,1)S(1)}, bf16[256,128]{1,0:T(8,128)(2,1)S(1)}, u32[]{:S(2)}, u32[]{:S(2)}) collective-permute-start(bf16[256,128]{1,0:T(8,128)(2,1)S(1)} %get-tuple-element.374), channel_id=1, source_target_pairs={{0,16},{16,32},{32,48},{48,64},{64,80},{80,96},{96,112},{112,128},... | collective-permute-start | bytes 196616 | tf_op jit(solution)/shard_map/while/body/eval_jaxpr/ppermute | solution.py:13
  91.5 8.3 %collective-permute-start.1 = (bf16[256,128]{1,0:T(8,128)(2,1)S(1)}, bf16[256,128]{1,0:T(8,128)(2,1)S(1)}, u32[]{:S(2)}, u32[]{:S(2)}) collective-permute-start(bf16[256,128]{1,0:T(8,128)(2,1)S(1)} %get-tuple-element.375), channel_id=1, source_target_pairs={{0,16},{16,32},{32,48},{48,64},{64,80},{80,96},{96,112},{112,128},... | collective-permute-start | bytes 196616 | tf_op jit(solution)/shard_map/while/body/eval_jaxpr/ppermute | solution.py:13
  93.4 8.9 %collective-permute-start = (bf16[256,128]{1,0:T(8,128)(2,1)S(1)}, bf16[256,128]{1,0:T(8,128)(2,1)S(1)}, u32[]{:S(2)}, u32[]{:S(2)}) collective-permute-start(bf16[256,128]{1,0:T(8,128)(2,1)S(1)} %get-tuple-element.374), channel_id=1, source_target_pairs={{0,16},{16,32},{32,48},{48,64},{64,80},{80,96},{96,112},{112,128},... | collective-permute-start | bytes 196616 | tf_op jit(solution)/shard_map/while/body/eval_jaxpr/ppermute | solution.py:13
  102.3 8.9 %collective-permute-start.1 = (bf16[256,128]{1,0:T(8,128)(2,1)S(1)}, bf16[256,128]{1,0:T(8,128)(2,1)S(1)}, u32[]{:S(2)}, u32[]{:S(2)}) collective-permute-start(bf16[256,128]{1,0:T(8,128)(2,1)S(1)} %get-tuple-element.375), channel_id=1, source_target_pairs={{0,16},{16,32},{32,48},{48,64},{64,80},{80,96},{96,112},{112,128},... | collective-permute-start | bytes 196616 | tf_op jit(solution)/shard_map/while/body/eval_jaxpr/ppermute | solution.py:13
  104.2 8.9 %collective-permute-start = (bf16[256,128]{1,0:T(8,128)(2,1)S(1)}, bf16[256,128]{1,0:T(8,128)(2,1)S(1)}, u32[]{:S(2)}, u32[]{:S(2)}) collective-permute-start(bf16[256,128]{1,0:T(8,128)(2,1)S(1)} %get-tuple-element.374), channel_id=1, source_target_pairs={{0,16},{16,32},{32,48},{48,64},{64,80},{80,96},{96,112},{112,128},... | collective-permute-start | bytes 196616 | tf_op jit(solution)/shard_map/while/body/eval_jaxpr/ppermute | solution.py:13
  113.2 8.3 %collective-permute-start.1 = (bf16[256,128]{1,0:T(8,128)(2,1)S(1)}, bf16[256,128]{1,0:T(8,128)(2,1)S(1)}, u32[]{:S(2)}, u32[]{:S(2)}) collective-permute-start(bf16[256,128]{1,0:T(8,128)(2,1)S(1)} %get-tuple-element.375), channel_id=1, source_target_pairs={{0,16},{16,32},{32,48},{48,64},{64,80},{80,96},{96,112},{112,128},... | collective-permute-start | bytes 196616 | tf_op jit(solution)/shard_map/while/body/eval_jaxpr/ppermute | solution.py:13
  115.1 8.3 %collective-permute-start = (bf16[256,128]{1,0:T(8,128)(2,1)S(1)}, bf16[256,128]{1,0:T(8,128)(2,1)S(1)}, u32[]{:S(2)}, u32[]{:S(2)}) collective-permute-start(bf16[256,128]{1,0:T(8,128)(2,1)S(1)} %get-tuple-element.374), channel_id=1, source_target_pairs={{0,16},{16,32},{32,48},{48,64},{64,80},{80,96},{96,112},{112,128},... | collective-permute-start | bytes 196616 | tf_op jit(solution)/shard_map/while/body/eval_jaxpr/ppermute | solution.py:13
  123.4 8.9 %collective-permute-start.1 = (bf16[256,128]{1,0:T(8,128)(2,1)S(1)}, bf16[256,128]{1,0:T(8,128)(2,1)S(1)}, u32[]{:S(2)}, u32[]{:S(2)}) collective-permute-start(bf16[256,128]{1,0:T(8,128)(2,1)S(1)} %get-tuple-element.375), channel_id=1, source_target_pairs={{0,16},{16,32},{32,48},{48,64},{64,80},{80,96},{96,112},{112,128},... | collective-permute-start | bytes 196616 | tf_op jit(solution)/shard_map/while/body/eval_jaxpr/ppermute | solution.py:13
  125.4 8.3 %collective-permute-start = (bf16[256,128]{1,0:T(8,128)(2,1)S(1)}, bf16[256,128]{1,0:T(8,128)(2,1)S(1)}, u32[]{:S(2)}, u32[]{:S(2)}) collective-permute-start(bf16[256,128]{1,0:T(8,128)(2,1)S(1)} %get-tuple-element.374), channel_id=1, source_target_pairs={{0,16},{16,32},{32,48},{48,64},{64,80},{80,96},{96,112},{112,128},... | collective-permute-start | bytes 196616 | tf_op jit(solution)/shard_map/while/body/eval_jaxpr/ppermute | solution.py:13
  133.7 8.7 %collective-permute-start.1 = (bf16[256,128]{1,0:T(8,128)(2,1)S(1)}, bf16[256,128]{1,0:T(8,128)(2,1)S(1)}, u32[]{:S(2)}, u32[]{:S(2)}) collective-permute-start(bf16[256,128]{1,0:T(8,128)(2,1)S(1)} %get-tuple-element.375), channel_id=1, source_target_pairs={{0,16},{16,32},{32,48},{48,64},{64,80},{80,96},{96,112},{112,128},... | collective-permute-start | bytes 196616 | tf_op jit(solution)/shard_map/while/body/eval_jaxpr/ppermute | solution.py:13
  135.6 8.3 %collective-permute-start = (bf16[256,128]{1,0:T(8,128)(2,1)S(1)}, bf16[256,128]{1,0:T(8,128)(2,1)S(1)}, u32[]{:S(2)}, u32[]{:S(2)}) collective-permute-start(bf16[256,128]{1,0:T(8,128)(2,1)S(1)} %get-tuple-element.374), channel_id=1, source_target_pairs={{0,16},{16,32},{32,48},{48,64},{64,80},{80,96},{96,112},{112,128},... | collective-permute-start | bytes 196616 | tf_op jit(solution)/shard_map/while/body/eval_jaxpr/ppermute | solution.py:13
  143.9 8.3 %collective-permute-start.1 = (bf16[256,128]{1,0:T(8,128)(2,1)S(1)}, bf16[256,128]{1,0:T(8,128)(2,1)S(1)}, u32[]{:S(2)}, u32[]{:S(2)}) collective-permute-start(bf16[256,128]{1,0:T(8,128)(2,1)S(1)} %get-tuple-element.375), channel_id=1, source_target_pairs={{0,16},{16,32},{32,48},{48,64},{64,80},{80,96},{96,112},{112,128},... | collective-permute-start | bytes 196616 | tf_op jit(solution)/shard_map/while/body/eval_jaxpr/ppermute | solution.py:13
  145.9 8.3 %collective-permute-start = (bf16[256,128]{1,0:T(8,128)(2,1)S(1)}, bf16[256,128]{1,0:T(8,128)(2,1)S(1)}, u32[]{:S(2)}, u32[]{:S(2)}) collective-permute-start(bf16[256,128]{1,0:T(8,128)(2,1)S(1)} %get-tuple-element.374), channel_id=1, source_target_pairs={{0,16},{16,32},{32,48},{48,64},{64,80},{80,96},{96,112},{112,128},... | collective-permute-start | bytes 196616 | tf_op jit(solution)/shard_map/while/body/eval_jaxpr/ppermute | solution.py:13
  154.2 8.3 %collective-permute-start.1 = (bf16[256,128]{1,0:T(8,128)(2,1)S(1)}, bf16[256,128]{1,0:T(8,128)(2,1)S(1)}, u32[]{:S(2)}, u32[]{:S(2)}) collective-permute-start(bf16[256,128]{1,0:T(8,128)(2,1)S(1)} %get-tuple-element.375), channel_id=1, source_target_pairs={{0,16},{16,32},{32,48},{48,64},{64,80},{80,96},{96,112},{112,128},... | collective-permute-start | bytes 196616 | tf_op jit(solution)/shard_map/while/body/eval_jaxpr/ppermute | solution.py:13
  156.1 8.3 %collective-permute-start = (bf16[256,128]{1,0:T(8,128)(2,1)S(1)}, bf16[256,128]{1,0:T(8,128)(2,1)S(1)}, u32[]{:S(2)}, u32[]{:S(2)}) collective-permute-start(bf16[256,128]{1,0:T(8,128)(2,1)S(1)} %get-tuple-element.374), channel_id=1, source_target_pairs={{0,16},{16,32},{32,48},{48,64},{64,80},{80,96},{96,112},{112,128},... | collective-permute-start | bytes 196616 | tf_op jit(solution)/shard_map/while/body/eval_jaxpr/ppermute | solution.py:13
  164.4 8.3 %collective-permute-start.1 = (bf16[256,128]{1,0:T(8,128)(2,1)S(1)}, bf16[256,128]{1,0:T(8,128)(2,1)S(1)}, u32[]{:S(2)}, u32[]{:S(2)}) collective-permute-start(bf16[256,128]{1,0:T(8,128)(2,1)S(1)} %get-tuple-element.375), channel_id=1, source_target_pairs={{0,16},{16,32},{32,48},{48,64},{64,80},{80,96},{96,112},{112,128},... | collective-permute-start | bytes 196616 | tf_op jit(solution)/shard_map/while/body/eval_jaxpr/ppermute | solution.py:13
  166.4 8.3 %collective-permute-start = (bf16[256,128]{1,0:T(8,128)(2,1)S(1)}, bf16[256,128]{1,0:T(8,128)(2,1)S(1)}, u32[]{:S(2)}, u32[]{:S(2)}) collective-permute-start(bf16[256,128]{1,0:T(8,128)(2,1)S(1)} %get-tuple-element.374), channel_id=1, source_target_pairs={{0,16},{16,32},{32,48},{48,64},{64,80},{80,96},{96,112},{112,128},... | collective-permute-start | bytes 196616 | tf_op jit(solution)/shard_map/while/body/eval_jaxpr/ppermute | solution.py:13
  174.7 8.3 %collective-permute-start.1 = (bf16[256,128]{1,0:T(8,128)(2,1)S(1)}, bf16[256,128]{1,0:T(8,128)(2,1)S(1)}, u32[]{:S(2)}, u32[]{:S(2)}) collective-permute-start(bf16[256,128]{1,0:T(8,128)(2,1)S(1)} %get-tuple-element.375), channel_id=1, source_target_pairs={{0,16},{16,32},{32,48},{48,64},{64,80},{80,96},{96,112},{112,128},... | collective-permute-start | bytes 196616 | tf_op jit(solution)/shard_map/while/body/eval_jaxpr/ppermute | solution.py:13
  176.6 8.3 %collective-permute-start = (bf16[256,128]{1,0:T(8,128)(2,1)S(1)}, bf16[256,128]{1,0:T(8,128)(2,1)S(1)}, u32[]{:S(2)}, u32[]{:S(2)}) collective-permute-start(bf16[256,128]{1,0:T(8,128)(2,1)S(1)} %get-tuple-element.374), channel_id=1, source_target_pairs={{0,16},{16,32},{32,48},{48,64},{64,80},{80,96},{96,112},{112,128},... | collective-permute-start | bytes 196616 | tf_op jit(solution)/shard_map/while/body/eval_jaxpr/ppermute | solution.py:13
  212.2 90.8 %all-gather.3.cloned.1.call-start = ((), (), s32[]{:S(2)}) async-start(), calls=%async_computation.4 | async-start | bytes 2785280 | tf_op jit(solution)/shard_map/all_gather | solution.py:109
  232.9 142.4 %reduce-scatter.4.cloned.1.call-start = ((), (), s32[]{:S(2)}) async-start(), calls=%async_computation.6 | async-start | bytes 2785280
  377.0 20.0 %all-to-all-start.2 = ((bf16[128,32,20]{0,2,1:T(8,128)(2,1)}), bf16[128,32,20]{0,2,1:T(8,128)(2,1)S(1)}, u32[]{:S(2)}, u32[]{:S(2)}) async-start(bf16[128,32,20]{0,2,1:T(8,128)(2,1)} %all_to_all.30), calls=%async_computation.2 | async-start | bytes 393216 | tf_op jit(solution)/shard_map/all_to_all | solution.py:130
  412.9 6.8 %collective-permute-start.3 = (bf16[256,128]{1,0:T(8,128)(2,1)S(1)}, bf16[256,128]{1,0:T(8,128)(2,1)S(1)}, u32[]{:S(2)}, u32[]{:S(2)}) collective-permute-start(bf16[256,128]{1,0:T(8,128)(2,1)S(1)} %get-tuple-element.398), channel_id=1, source_target_pairs={{16,0},{32,16},{48,32},{64,48},{80,64},{96,80},{112,96},{128,112},... | collective-permute-start | bytes 196616 | tf_op jit(solution)/shard_map/while/body/eval_jaxpr/ppermute | solution.py:13
  422.3 7.7 %collective-permute-start.3 = (bf16[256,128]{1,0:T(8,128)(2,1)S(1)}, bf16[256,128]{1,0:T(8,128)(2,1)S(1)}, u32[]{:S(2)}, u32[]{:S(2)}) collective-permute-start(bf16[256,128]{1,0:T(8,128)(2,1)S(1)} %get-tuple-element.398), channel_id=1, source_target_pairs={{16,0},{32,16},{48,32},{64,48},{80,64},{96,80},{112,96},{128,112},... | collective-permute-start | bytes 196616 | tf_op jit(solution)/shard_map/while/body/eval_jaxpr/ppermute | solution.py:13
  428.0 6.2 %collective-permute-start.2 = (bf16[256,128]{1,0:T(8,128)(2,1)S(1)}, bf16[256,128]{1,0:T(8,128)(2,1)S(1)}, u32[]{:S(2)}, u32[]{:S(2)}) collective-permute-start(bf16[256,128]{1,0:T(8,128)(2,1)S(1)} %get-tuple-element.397), channel_id=1, source_target_pairs={{16,0},{32,16},{48,32},{64,48},{80,64},{96,80},{112,96},{128,112},... | collective-permute-start | bytes 196616 | tf_op jit(solution)/shard_map/while/body/eval_jaxpr/ppermute | solution.py:13
  434.2 6.2 %collective-permute-start.3 = (bf16[256,128]{1,0:T(8,128)(2,1)S(1)}, bf16[256,128]{1,0:T(8,128)(2,1)S(1)}, u32[]{:S(2)}, u32[]{:S(2)}) collective-permute-start(bf16[256,128]{1,0:T(8,128)(2,1)S(1)} %get-tuple-element.398), channel_id=1, source_target_pairs={{16,0},{32,16},{48,32},{64,48},{80,64},{96,80},{112,96},{128,112},... | collective-permute-start | bytes 196616 | tf_op jit(solution)/shard_map/while/body/eval_jaxpr/ppermute | solution.py:13
  444.6 6.6 %collective-permute-start.3 = (bf16[256,128]{1,0:T(8,128)(2,1)S(1)}, bf16[256,128]{1,0:T(8,128)(2,1)S(1)}, u32[]{:S(2)}, u32[]{:S(2)}) collective-permute-start(bf16[256,128]{1,0:T(8,128)(2,1)S(1)} %get-tuple-element.398), channel_id=1, source_target_pairs={{16,0},{32,16},{48,32},{64,48},{80,64},{96,80},{112,96},{128,112},... | collective-permute-start | bytes 196616 | tf_op jit(solution)/shard_map/while/body/eval_jaxpr/ppermute | solution.py:13
  448.6 6.6 %collective-permute-start.2 = (bf16[256,128]{1,0:T(8,128)(2,1)S(1)}, bf16[256,128]{1,0:T(8,128)(2,1)S(1)}, u32[]{:S(2)}, u32[]{:S(2)}) collective-permute-start(bf16[256,128]{1,0:T(8,128)(2,1)S(1)} %get-tuple-element.397), channel_id=1, source_target_pairs={{16,0},{32,16},{48,32},{64,48},{80,64},{96,80},{112,96},{128,112},... | collective-permute-start | bytes 196616 | tf_op jit(solution)/shard_map/while/body/eval_jaxpr/ppermute | solution.py:13
  465.7 6.4 %collective-permute-start.3 = (bf16[256,128]{1,0:T(8,128)(2,1)S(1)}, bf16[256,128]{1,0:T(8,128)(2,1)S(1)}, u32[]{:S(2)}, u32[]{:S(2)}) collective-permute-start(bf16[256,128]{1,0:T(8,128)(2,1)S(1)} %get-tuple-element.398), channel_id=1, source_target_pairs={{16,0},{32,16},{48,32},{64,48},{80,64},{96,80},{112,96},{128,112},... | collective-permute-start | bytes 196616 | tf_op jit(solution)/shard_map/while/body/eval_jaxpr/ppermute | solution.py:13
  475.9 6.2 %collective-permute-start.3 = (bf16[256,128]{1,0:T(8,128)(2,1)S(1)}, bf16[256,128]{1,0:T(8,128)(2,1)S(1)}, u32[]{:S(2)}, u32[]{:S(2)}) collective-permute-start(bf16[256,128]{1,0:T(8,128)(2,1)S(1)} %get-tuple-element.398), channel_id=1, source_target_pairs={{16,0},{32,16},{48,32},{64,48},{80,64},{96,80},{112,96},{128,112},... | collective-permute-start | bytes 196616 | tf_op jit(solution)/shard_map/while/body/eval_jaxpr/ppermute | solution.py:13
  496.4 6.8 %collective-permute-start.3 = (bf16[256,128]{1,0:T(8,128)(2,1)S(1)}, bf16[256,128]{1,0:T(8,128)(2,1)S(1)}, u32[]{:S(2)}, u32[]{:S(2)}) collective-permute-start(bf16[256,128]{1,0:T(8,128)(2,1)S(1)} %get-tuple-element.398), channel_id=1, source_target_pairs={{16,0},{32,16},{48,32},{64,48},{80,64},{96,80},{112,96},{128,112},... | collective-permute-start | bytes 196616 | tf_op jit(solution)/shard_map/while/body/eval_jaxpr/ppermute | solution.py:13
  510.7 6.6 %collective-permute-start.2 = (bf16[256,128]{1,0:T(8,128)(2,1)S(1)}, bf16[256,128]{1,0:T(8,128)(2,1)S(1)}, u32[]{:S(2)}, u32[]{:S(2)}) collective-permute-start(bf16[256,128]{1,0:T(8,128)(2,1)S(1)} %get-tuple-element.397), channel_id=1, source_target_pairs={{16,0},{32,16},{48,32},{64,48},{80,64},{96,80},{112,96},{128,112},... | collective-permute-start | bytes 196616 | tf_op jit(solution)/shard_map/while/body/eval_jaxpr/ppermute | solution.py:13
  537.3 7.0 %collective-permute-start.3 = (bf16[256,128]{1,0:T(8,128)(2,1)S(1)}, bf16[256,128]{1,0:T(8,128)(2,1)S(1)}, u32[]{:S(2)}, u32[]{:S(2)}) collective-permute-start(bf16[256,128]{1,0:T(8,128)(2,1)S(1)} %get-tuple-element.398), channel_id=1, source_target_pairs={{16,0},{32,16},{48,32},{64,48},{80,64},{96,80},{112,96},{128,112},... | collective-permute-start | bytes 196616 | tf_op jit(solution)/shard_map/while/body/eval_jaxpr/ppermute | solution.py:13
  541.9 6.7 %collective-permute-start.2 = (bf16[256,128]{1,0:T(8,128)(2,1)S(1)}, bf16[256,128]{1,0:T(8,128)(2,1)S(1)}, u32[]{:S(2)}, u32[]{:S(2)}) collective-permute-start(bf16[256,128]{1,0:T(8,128)(2,1)S(1)} %get-tuple-element.397), channel_id=1, source_target_pairs={{16,0},{32,16},{48,32},{64,48},{80,64},{96,80},{112,96},{128,112},... | collective-permute-start | bytes 196616 | tf_op jit(solution)/shard_map/while/body/eval_jaxpr/ppermute | solution.py:13
  (30 other events, 405.7 us)
Sparse Core Ops, SparseCore 0:
  212.3 43.3 all-gather.4
  258.4 44.5 all-gather.2
  313.7 61.4 reduce-scatter.3
where the time goes:
time: 590 us; the launch traced here: 587 us
  waiting for transfers between devices  277 us (47%)
  starting transfers between devices  183 us (31%)
  matrix products  35.4 us (6%)
  blocking collectives  31.8 us (5%)
  local copies, waits for them, and re-layouts  21.9 us (4%)
  other arithmetic  21.3 us (4%)
  between operations  14.7 us (2%)
    ppermute x64, starting transfers between devices, shifted(): return lax.ppermute(block, axis, route)  173 us
    ppermute x64, waiting for transfers between devices, shifted(): return lax.ppermute(block, axis, route)  147 us
    unnamed x4, waiting for transfers between devices  57.7 us
    all_gather x1, waiting for transfers between devices, per_device(): full_grads = lax.all_gather(recv_grads, 'exp', axis=1, tiled=True)  43.8 us
    all_gather x1, waiting for transfers between devices, per_device(): full_tokens = lax.all_gather(recv_tokens, 'exp', axis=1, tiled=True)  22.8 us
    all_to_all x1, blocking collectives, per_device(): lax.all_to_all(send_grads, 'seq', split_axis=0, concat_axis=0, tiled=True)  15.9 us
    all_to_all x1, blocking collectives, per_device(): lax.all_to_all(send_tokens, 'seq', split_axis=0, concat_axis=0, tiled=True)  15.8 us
    add x16, other arithmetic, relay_grads(): value_acc + lax.dynamic_index_in_dim(value_parts, index, 0, keepdims=False)  14.7 us
  transfers between devices with their start and end apart: 68, of which 64 were waited for; matrix products, arithmetic and copies ran while one was open for 5% of the time, Pallas kernels for 0%

commit v1 on v0

--- a/solution.py
+++ b/solution.py
@@ -104,7 +104,12 @@
     )
     weight_in = expert_in[0]
     weight_out = expert_out[0]
-    full_tokens = lax.all_gather(recv_tokens, "exp", axis=1, tiled=True)
+    ring = [recv_tokens]
+    for hop in range(15):
+        ring.append(lax.ppermute(ring[-1], "exp", [(dev, (dev + 1) % 16) for dev in range(16)]))
+    full_tokens = jnp.roll(
+        jnp.concatenate(ring[::-1], axis=1), (lax.axis_index("exp") + 1) * ring[0].shape[1], axis=1
+    )
     pre_act = jnp.dot(full_tokens, weight_in, preferred_element_type=jnp.float32)
     full_grads = lax.all_gather(recv_grads, "exp", axis=1, tiled=True)
     logistic = jax.nn.sigmoid(pre_act)

time: 590 us -> 628 us (1.064)
  waiting for transfers between devices: 277 us -> 315 us
  blocking collectives: 31.8 us -> 15.6 us
  local copies, waits for them, and re-layouts: 21.9 us -> 36.9 us
    ppermute x0 -> x15, waiting for transfers between devices: none -> 83.1 us  [per_device(): lax.ppermute(ring[-1], 'exp', [(dev, (dev + 1) % 16) for dev in range(16)])]
    all_gather x1, waiting for transfers between devices: 43.8 us -> 0.02 us  [per_device(): full_grads = lax.all_gather(recv_grads, 'exp', axis=1, tiled=True)]
    all_gather x1 -> x0, waiting for transfers between devices: 22.8 us -> none  [per_device(): full_tokens = lax.all_gather(recv_tokens, 'exp', axis=1, tiled=True)]
    unnamed x26 -> x73, local copies, waits for them, and re-layouts: 10 us -> 28.4 us
    all_to_all x1 -> x0, blocking collectives: 15.9 us -> none  [per_device(): lax.all_to_all(send_grads, 'seq', split_axis=0, concat_axis=0, tiled=True)]
    ppermute x64, waiting for transfers between devices: 147 us -> 161 us  [shifted(): return lax.ppermute(block, axis, route)]
    unnamed x4 -> x3, waiting for transfers between devices: 57.7 us -> 62.5 us
  transfers between devices with their start and end apart: 68 -> 83, of which waited for: 64 -> 76; matrix products, arithmetic and copies ran while one was open for 5% -> 4% of each run, Pallas kernels for 0% -> 0%
where the time goes in v1:
time: 628 us; the launch traced here: 625 us
  waiting for transfers between devices  315 us (50%)
  starting transfers between devices  189 us (30%)
  local copies, waits for them, and re-layouts  36.9 us (6%)
  matrix products  31 us (5%)
  other arithmetic  20.4 us (3%)
  blocking collectives  15.6 us (2%)
  between operations  15.3 us (2%)
    ppermute x64, starting transfers between devices, shifted(): return lax.ppermute(block, axis, route)  172 us
    ppermute x64, waiting for transfers between devices, shifted(): return lax.ppermute(block, axis, route)  161 us
    ppermute x15, waiting for transfers between devices, per_device(): lax.ppermute(ring[-1], 'exp', [(dev, (dev + 1) % 16) for dev in range(16)])  83.1 us
    unnamed x3, waiting for transfers between devices  62.5 us
    unnamed x73, local copies, waits for them, and re-layouts  28.4 us
    all_to_all x1, blocking collectives, per_device(): lax.all_to_all(send_tokens, 'seq', split_axis=0, concat_axis=0, tiled=True)  15.6 us
    add x16, other arithmetic, relay_grads(): value_acc + lax.dynamic_index_in_dim(value_parts, index, 0, keepdims=False)  14.7 us
  transfers between devices with their start and end apart: 83, of which 76 were waited for; matrix products, arithmetic and copies ran while one was open for 4% of the time, Pallas kernels for 0%

profile of v1, /device:TPU:2, one launch (start us, length us, event | category | flops | bytes accessed | tf_op | source)
XLA Modules:
  0.0 624.7 jit_solution(6289347989920543827)
XLA Ops:
  14.7 170.1 %while.36 = (s32[]{:T(128)}, bf16[17,256,128]{2,1,0:T(8,128)(2,1)S(1)}, bf16[17,256,128]{2,1,0:T(8,128)(2,1)S(1)}, bf16[256,128]{1,0:T(8,128)(2,1)S(1)}, bf16[25...) while((s32[]{:T(128)}, bf16[17,256,128]{2,1,0:T(8,128)(2,1)S(1)}, ...), condition=%wide.region_1.2_spmd, body=%wide.region_0.1_spmd.sunk | while | flops 5 | bytes 1048791 | solution.py:74
  14.7 4.3 collective-permute-start
  19.0 4.3 collective-permute-start.1
  23.3 4.6 collective-permute-done
  85.0 4.4 collective-permute-done
  95.2 4.4 collective-permute-done
  106.1 5.0 collective-permute-done
  116.9 4.4 collective-permute-done
  127.2 5.0 collective-permute-done
  137.4 4.8 collective-permute-done
  147.7 4.4 collective-permute-done
  157.9 4.4 collective-permute-done
  168.2 4.4 collective-permute-done
  178.4 4.4 collective-permute-done
  184.8 6.0 fusion.74
  194.0 15.6 %all_to_all.36 = bf16[32,20,128]{2,1,0:T(8,128)(2,1)S(1)} all-to-all(bf16[32,20,128]{2,1,0:T(8,128)(2,1)S(1)} %all_to_all.27), channel_id=1, replica_groups=mesh['seq'=32,'exp'=16] {'seq'}, dimensions={0} | all-to-all | bytes 327680 | tf_op jit(solution)/shard_map/all_to_all | solution.py:102
  209.7 5.9 collective-permute-done.4
  215.7 6.0 collective-permute-done.5
  221.6 6.0 collective-permute-done.6
  227.6 6.0 collective-permute-done.7
  233.5 6.0 collective-permute-done.8
  239.5 5.9 collective-permute-done.9
  246.4 5.1 collective-permute-done.10
  252.6 5.4 all-to-all-start
  258.1 6.3 %collective-permute-done.12 = bf16[640,128]{1,0:T(8,128)(2,1)} collective-permute-done((bf16[640,128]{1,0:T(8,128)(2,1)}, bf16[640,128]{1,0:T(8,128)(2,1)}, u32[]{:S(2)}, u32[]{:S(2)}) %collective-permute-start.12) | collective-permute-done | bytes 163872 | tf_op jit(solution)/shard_map/ppermute | solution.py:109
  270.7 6.2 collective-permute-done.14
  276.8 6.0 collective-permute-done.15
  283.4 7.7 %collective-permute-done.16 = bf16[640,128]{1,0:T(8,128)(2,1)S(1)} collective-permute-done((bf16[640,128]{1,0:T(8,128)(2,1)S(1)}, bf16[640,128]{1,0:T(8,128)(2,1)S(1)}, u32[]{:S(2)}, u32[]{:S(2)}) %collective-permute-start.16) | collective-permute-done | bytes 163872 | tf_op jit(solution)/shard_map/ppermute | solution.py:109
  291.8 6.9 %collective-permute-done.17 = bf16[640,128]{1,0:T(8,128)(2,1)} collective-permute-done((bf16[640,128]{1,0:T(8,128)(2,1)S(1)}, bf16[640,128]{1,0:T(8,128)(2,1)}, u32[]{:S(2)}, u32[]{:S(2)}) %collective-permute-start.17) | collective-permute-done | bytes 163872 | tf_op jit(solution)/shard_map/ppermute | solution.py:109
  298.8 7.0 %collective-permute-done.18 = bf16[640,128]{1,0:T(8,128)(2,1)} collective-permute-done((bf16[640,128]{1,0:T(8,128)(2,1)}, bf16[640,128]{1,0:T(8,128)(2,1)}, u32[]{:S(2)}, u32[]{:S(2)}) %collective-permute-start.18) | collective-permute-done | bytes 163872 | tf_op jit(solution)/shard_map/ppermute | solution.py:109
  329.0 4.4 copy.33
  337.2 62.5 %reduce-scatter.4.cloned.1.call-done = bf16[128,640]{1,0:T(8,128)(2,1)} async-done(((bf16[2048,640]{1,0:T(8,128)(2,1)}), bf16[128,640]{1,0:T(8,128)(2,1)}) %reduce-scatter.4.cloned.1.call-update) | async-done | bytes 163856
  401.5 10.5 %all-to-all-start.2 = ((bf16[128,32,20]{0,2,1:T(8,128)(2,1)}), bf16[128,32,20]{0,2,1:T(8,128)(2,1)S(1)}, u32[]{:S(2)}, u32[]{:S(2)}) async-start(bf16[128,32,20]{0,2,1:T(8,128)(2,1)} %all_to_all.30), calls=%async_computation.2 | async-start | bytes 393216 | tf_op jit(solution)/shard_map/all_to_all | solution.py:135
  415.7 5.7 all-to-all-done.2
  422.1 4.6 convolution_bitcast_fusion
  436.7 180.5 %while.37 = (s32[]{:T(128)}, bf16[256,128]{1,0:T(8,128)(2,1)S(1)}, bf16[256,128]{1,0:T(8,128)(2,1)S(1)}, f32[17,256,128]{2,1,0:T(8,128)S(1)}, f32[17,256,128]{2,...) while((s32[]{:T(128)}, bf16[256,128]{1,0:T(8,128)(2,1)S(1)}, ...), condition=%wide.region_9.10_spmd, body=%wide.region_8.9_spmd.sunk | while | flops 196614 | bytes 1048803 | solution.py:171
  447.4 5.4 collective-permute-start.2
  454.7 4.2 collective-permute-done.3
  459.9 4.0 collective-permute-start.2
  471.0 4.5 collective-permute-start.2
  477.4 4.5 collective-permute-done.3
  493.7 4.3 collective-permute-start.2
  500.0 4.2 collective-permute-done.3
  544.7 4.3 collective-permute-done.3
  571.9 4.2 collective-permute-start.2
  578.1 4.2 collective-permute-done.3
  594.8 4.2 collective-permute-start.2
  601.0 4.1 collective-permute-done.3
  (340 shorter events, 301.6 us)
Async XLA Ops:
  14.7 13.2 %collective-permute-start = (bf16[256,128]{1,0:T(8,128)(2,1)S(1)}, bf16[256,128]{1,0:T(8,128)(2,1)S(1)}, u32[]{:S(2)}, u32[]{:S(2)}) collective-permute-start(bf16[256,128]{1,0:T(8,128)(2,1)S(1)} %get-tuple-element.374), channel_id=1, source_target_pairs={{0,16},{16,32},{32,48},{48,64},{64,80},{80,96},{96,112},{112,128},... | collective-permute-start | bytes 196616 | tf_op jit(solution)/shard_map/while/body/eval_jaxpr/ppermute | solution.py:13
  19.0 10.8 %collective-permute-start.1 = (bf16[256,128]{1,0:T(8,128)(2,1)S(1)}, bf16[256,128]{1,0:T(8,128)(2,1)S(1)}, u32[]{:S(2)}, u32[]{:S(2)}) collective-permute-start(bf16[256,128]{1,0:T(8,128)(2,1)S(1)} %get-tuple-element.375), channel_id=1, source_target_pairs={{0,16},{16,32},{32,48},{48,64},{64,80},{80,96},{96,112},{112,128},... | collective-permute-start | bytes 196616 | tf_op jit(solution)/shard_map/while/body/eval_jaxpr/ppermute | solution.py:13
  29.9 8.9 %collective-permute-start = (bf16[256,128]{1,0:T(8,128)(2,1)S(1)}, bf16[256,128]{1,0:T(8,128)(2,1)S(1)}, u32[]{:S(2)}, u32[]{:S(2)}) collective-permute-start(bf16[256,128]{1,0:T(8,128)(2,1)S(1)} %get-tuple-element.374), channel_id=1, source_target_pairs={{0,16},{16,32},{32,48},{48,64},{64,80},{80,96},{96,112},{112,128},... | collective-permute-start | bytes 196616 | tf_op jit(solution)/shard_map/while/body/eval_jaxpr/ppermute | solution.py:13
  31.8 8.3 %collective-permute-start.1 = (bf16[256,128]{1,0:T(8,128)(2,1)S(1)}, bf16[256,128]{1,0:T(8,128)(2,1)S(1)}, u32[]{:S(2)}, u32[]{:S(2)}) collective-permute-start(bf16[256,128]{1,0:T(8,128)(2,1)S(1)} %get-tuple-element.375), channel_id=1, source_target_pairs={{0,16},{16,32},{32,48},{48,64},{64,80},{80,96},{96,112},{112,128},... | collective-permute-start | bytes 196616 | tf_op jit(solution)/shard_map/while/body/eval_jaxpr/ppermute | solution.py:13
  40.1 8.7 %collective-permute-start = (bf16[256,128]{1,0:T(8,128)(2,1)S(1)}, bf16[256,128]{1,0:T(8,128)(2,1)S(1)}, u32[]{:S(2)}, u32[]{:S(2)}) collective-permute-start(bf16[256,128]{1,0:T(8,128)(2,1)S(1)} %get-tuple-element.374), channel_id=1, source_target_pairs={{0,16},{16,32},{32,48},{48,64},{64,80},{80,96},{96,112},{112,128},... | collective-permute-start | bytes 196616 | tf_op jit(solution)/shard_map/while/body/eval_jaxpr/ppermute | solution.py:13
  42.0 8.3 %collective-permute-start.1 = (bf16[256,128]{1,0:T(8,128)(2,1)S(1)}, bf16[256,128]{1,0:T(8,128)(2,1)S(1)}, u32[]{:S(2)}, u32[]{:S(2)}) collective-permute-start(bf16[256,128]{1,0:T(8,128)(2,1)S(1)} %get-tuple-element.375), channel_id=1, source_target_pairs={{0,16},{16,32},{32,48},{48,64},{64,80},{80,96},{96,112},{112,128},... | collective-permute-start | bytes 196616 | tf_op jit(solution)/shard_map/while/body/eval_jaxpr/ppermute | solution.py:13
  50.4 8.3 %collective-permute-start = (bf16[256,128]{1,0:T(8,128)(2,1)S(1)}, bf16[256,128]{1,0:T(8,128)(2,1)S(1)}, u32[]{:S(2)}, u32[]{:S(2)}) collective-permute-start(bf16[256,128]{1,0:T(8,128)(2,1)S(1)} %get-tuple-element.374), channel_id=1, source_target_pairs={{0,16},{16,32},{32,48},{48,64},{64,80},{80,96},{96,112},{112,128},... | collective-permute-start | bytes 196616 | tf_op jit(solution)/shard_map/while/body/eval_jaxpr/ppermute | solution.py:13
  52.3 8.3 %collective-permute-start.1 = (bf16[256,128]{1,0:T(8,128)(2,1)S(1)}, bf16[256,128]{1,0:T(8,128)(2,1)S(1)}, u32[]{:S(2)}, u32[]{:S(2)}) collective-permute-start(bf16[256,128]{1,0:T(8,128)(2,1)S(1)} %get-tuple-element.375), channel_id=1, source_target_pairs={{0,16},{16,32},{32,48},{48,64},{64,80},{80,96},{96,112},{112,128},... | collective-permute-start | bytes 196616 | tf_op jit(solution)/shard_map/while/body/eval_jaxpr/ppermute | solution.py:13
  60.6 8.3 %collective-permute-start = (bf16[256,128]{1,0:T(8,128)(2,1)S(1)}, bf16[256,128]{1,0:T(8,128)(2,1)S(1)}, u32[]{:S(2)}, u32[]{:S(2)}) collective-permute-start(bf16[256,128]{1,0:T(8,128)(2,1)S(1)} %get-tuple-element.374), channel_id=1, source_target_pairs={{0,16},{16,32},{32,48},{48,64},{64,80},{80,96},{96,112},{112,128},... | collective-permute-start | bytes 196616 | tf_op jit(solution)/shard_map/while/body/eval_jaxpr/ppermute | solution.py:13
  62.5 8.3 %collective-permute-start.1 = (bf16[256,128]{1,0:T(8,128)(2,1)S(1)}, bf16[256,128]{1,0:T(8,128)(2,1)S(1)}, u32[]{:S(2)}, u32[]{:S(2)}) collective-permute-start(bf16[256,128]{1,0:T(8,128)(2,1)S(1)} %get-tuple-element.375), channel_id=1, source_target_pairs={{0,16},{16,32},{32,48},{48,64},{64,80},{80,96},{96,112},{112,128},... | collective-permute-start | bytes 196616 | tf_op jit(solution)/shard_map/while/body/eval_jaxpr/ppermute | solution.py:13
  70.9 8.3 %collective-permute-start = (bf16[256,128]{1,0:T(8,128)(2,1)S(1)}, bf16[256,128]{1,0:T(8,128)(2,1)S(1)}, u32[]{:S(2)}, u32[]{:S(2)}) collective-permute-start(bf16[256,128]{1,0:T(8,128)(2,1)S(1)} %get-tuple-element.374), channel_id=1, source_target_pairs={{0,16},{16,32},{32,48},{48,64},{64,80},{80,96},{96,112},{112,128},... | collective-permute-start | bytes 196616 | tf_op jit(solution)/shard_map/while/body/eval_jaxpr/ppermute | solution.py:13
  72.8 8.3 %collective-permute-start.1 = (bf16[256,128]{1,0:T(8,128)(2,1)S(1)}, bf16[256,128]{1,0:T(8,128)(2,1)S(1)}, u32[]{:S(2)}, u32[]{:S(2)}) collective-permute-start(bf16[256,128]{1,0:T(8,128)(2,1)S(1)} %get-tuple-element.375), channel_id=1, source_target_pairs={{0,16},{16,32},{32,48},{48,64},{64,80},{80,96},{96,112},{112,128},... | collective-permute-start | bytes 196616 | tf_op jit(solution)/shard_map/while/body/eval_jaxpr/ppermute | solution.py:13
  81.1 8.3 %collective-permute-start = (bf16[256,128]{1,0:T(8,128)(2,1)S(1)}, bf16[256,128]{1,0:T(8,128)(2,1)S(1)}, u32[]{:S(2)}, u32[]{:S(2)}) collective-permute-start(bf16[256,128]{1,0:T(8,128)(2,1)S(1)} %get-tuple-element.374), channel_id=1, source_target_pairs={{0,16},{16,32},{32,48},{48,64},{64,80},{80,96},{96,112},{112,128},... | collective-permute-start | bytes 196616 | tf_op jit(solution)/shard_map/while/body/eval_jaxpr/ppermute | solution.py:13
  83.1 8.3 %collective-permute-start.1 = (bf16[256,128]{1,0:T(8,128)(2,1)S(1)}, bf16[256,128]{1,0:T(8,128)(2,1)S(1)}, u32[]{:S(2)}, u32[]{:S(2)}) collective-permute-start(bf16[256,128]{1,0:T(8,128)(2,1)S(1)} %get-tuple-element.375), channel_id=1, source_target_pairs={{0,16},{16,32},{32,48},{48,64},{64,80},{80,96},{96,112},{112,128},... | collective-permute-start | bytes 196616 | tf_op jit(solution)/shard_map/while/body/eval_jaxpr/ppermute | solution.py:13
  91.4 8.3 %collective-permute-start = (bf16[256,128]{1,0:T(8,128)(2,1)S(1)}, bf16[256,128]{1,0:T(8,128)(2,1)S(1)}, u32[]{:S(2)}, u32[]{:S(2)}) collective-permute-start(bf16[256,128]{1,0:T(8,128)(2,1)S(1)} %get-tuple-element.374), channel_id=1, source_target_pairs={{0,16},{16,32},{32,48},{48,64},{64,80},{80,96},{96,112},{112,128},... | collective-permute-start | bytes 196616 | tf_op jit(solution)/shard_map/while/body/eval_jaxpr/ppermute | solution.py:13
  93.3 8.9 %collective-permute-start.1 = (bf16[256,128]{1,0:T(8,128)(2,1)S(1)}, bf16[256,128]{1,0:T(8,128)(2,1)S(1)}, u32[]{:S(2)}, u32[]{:S(2)}) collective-permute-start(bf16[256,128]{1,0:T(8,128)(2,1)S(1)} %get-tuple-element.375), channel_id=1, source_target_pairs={{0,16},{16,32},{32,48},{48,64},{64,80},{80,96},{96,112},{112,128},... | collective-permute-start | bytes 196616 | tf_op jit(solution)/shard_map/while/body/eval_jaxpr/ppermute | solution.py:13
  102.2 8.9 %collective-permute-start = (bf16[256,128]{1,0:T(8,128)(2,1)S(1)}, bf16[256,128]{1,0:T(8,128)(2,1)S(1)}, u32[]{:S(2)}, u32[]{:S(2)}) collective-permute-start(bf16[256,128]{1,0:T(8,128)(2,1)S(1)} %get-tuple-element.374), channel_id=1, source_target_pairs={{0,16},{16,32},{32,48},{48,64},{64,80},{80,96},{96,112},{112,128},... | collective-permute-start | bytes 196616 | tf_op jit(solution)/shard_map/while/body/eval_jaxpr/ppermute | solution.py:13
  104.1 8.9 %collective-permute-start.1 = (bf16[256,128]{1,0:T(8,128)(2,1)S(1)}, bf16[256,128]{1,0:T(8,128)(2,1)S(1)}, u32[]{:S(2)}, u32[]{:S(2)}) collective-permute-start(bf16[256,128]{1,0:T(8,128)(2,1)S(1)} %get-tuple-element.375), channel_id=1, source_target_pairs={{0,16},{16,32},{32,48},{48,64},{64,80},{80,96},{96,112},{112,128},... | collective-permute-start | bytes 196616 | tf_op jit(solution)/shard_map/while/body/eval_jaxpr/ppermute | solution.py:13
  113.1 8.3 %collective-permute-start = (bf16[256,128]{1,0:T(8,128)(2,1)S(1)}, bf16[256,128]{1,0:T(8,128)(2,1)S(1)}, u32[]{:S(2)}, u32[]{:S(2)}) collective-permute-start(bf16[256,128]{1,0:T(8,128)(2,1)S(1)} %get-tuple-element.374), channel_id=1, source_target_pairs={{0,16},{16,32},{32,48},{48,64},{64,80},{80,96},{96,112},{112,128},... | collective-permute-start | bytes 196616 | tf_op jit(solution)/shard_map/while/body/eval_jaxpr/ppermute | solution.py:13
  115.0 8.3 %collective-permute-start.1 = (bf16[256,128]{1,0:T(8,128)(2,1)S(1)}, bf16[256,128]{1,0:T(8,128)(2,1)S(1)}, u32[]{:S(2)}, u32[]{:S(2)}) collective-permute-start(bf16[256,128]{1,0:T(8,128)(2,1)S(1)} %get-tuple-element.375), channel_id=1, source_target_pairs={{0,16},{16,32},{32,48},{48,64},{64,80},{80,96},{96,112},{112,128},... | collective-permute-start | bytes 196616 | tf_op jit(solution)/shard_map/while/body/eval_jaxpr/ppermute | solution.py:13
  123.3 8.9 %collective-permute-start = (bf16[256,128]{1,0:T(8,128)(2,1)S(1)}, bf16[256,128]{1,0:T(8,128)(2,1)S(1)}, u32[]{:S(2)}, u32[]{:S(2)}) collective-permute-start(bf16[256,128]{1,0:T(8,128)(2,1)S(1)} %get-tuple-element.374), channel_id=1, source_target_pairs={{0,16},{16,32},{32,48},{48,64},{64,80},{80,96},{96,112},{112,128},... | collective-permute-start | bytes 196616 | tf_op jit(solution)/shard_map/while/body/eval_jaxpr/ppermute | solution.py:13
  125.3 8.3 %collective-permute-start.1 = (bf16[256,128]{1,0:T(8,128)(2,1)S(1)}, bf16[256,128]{1,0:T(8,128)(2,1)S(1)}, u32[]{:S(2)}, u32[]{:S(2)}) collective-permute-start(bf16[256,128]{1,0:T(8,128)(2,1)S(1)} %get-tuple-element.375), channel_id=1, source_target_pairs={{0,16},{16,32},{32,48},{48,64},{64,80},{80,96},{96,112},{112,128},... | collective-permute-start | bytes 196616 | tf_op jit(solution)/shard_map/while/body/eval_jaxpr/ppermute | solution.py:13
  133.6 8.7 %collective-permute-start = (bf16[256,128]{1,0:T(8,128)(2,1)S(1)}, bf16[256,128]{1,0:T(8,128)(2,1)S(1)}, u32[]{:S(2)}, u32[]{:S(2)}) collective-permute-start(bf16[256,128]{1,0:T(8,128)(2,1)S(1)} %get-tuple-element.374), channel_id=1, source_target_pairs={{0,16},{16,32},{32,48},{48,64},{64,80},{80,96},{96,112},{112,128},... | collective-permute-start | bytes 196616 | tf_op jit(solution)/shard_map/while/body/eval_jaxpr/ppermute | solution.py:13
  135.5 8.3 %collective-permute-start.1 = (bf16[256,128]{1,0:T(8,128)(2,1)S(1)}, bf16[256,128]{1,0:T(8,128)(2,1)S(1)}, u32[]{:S(2)}, u32[]{:S(2)}) collective-permute-start(bf16[256,128]{1,0:T(8,128)(2,1)S(1)} %get-tuple-element.375), channel_id=1, source_target_pairs={{0,16},{16,32},{32,48},{48,64},{64,80},{80,96},{96,112},{112,128},... | collective-permute-start | bytes 196616 | tf_op jit(solution)/shard_map/while/body/eval_jaxpr/ppermute | solution.py:13
  143.8 8.3 %collective-permute-start = (bf16[256,128]{1,0:T(8,128)(2,1)S(1)}, bf16[256,128]{1,0:T(8,128)(2,1)S(1)}, u32[]{:S(2)}, u32[]{:S(2)}) collective-permute-start(bf16[256,128]{1,0:T(8,128)(2,1)S(1)} %get-tuple-element.374), channel_id=1, source_target_pairs={{0,16},{16,32},{32,48},{48,64},{64,80},{80,96},{96,112},{112,128},... | collective-permute-start | bytes 196616 | tf_op jit(solution)/shard_map/while/body/eval_jaxpr/ppermute | solution.py:13
  145.8 8.3 %collective-permute-start.1 = (bf16[256,128]{1,0:T(8,128)(2,1)S(1)}, bf16[256,128]{1,0:T(8,128)(2,1)S(1)}, u32[]{:S(2)}, u32[]{:S(2)}) collective-permute-start(bf16[256,128]{1,0:T(8,128)(2,1)S(1)} %get-tuple-element.375), channel_id=1, source_target_pairs={{0,16},{16,32},{32,48},{48,64},{64,80},{80,96},{96,112},{112,128},... | collective-permute-start | bytes 196616 | tf_op jit(solution)/shard_map/while/body/eval_jaxpr/ppermute | solution.py:13
  154.1 8.3 %collective-permute-start = (bf16[256,128]{1,0:T(8,128)(2,1)S(1)}, bf16[256,128]{1,0:T(8,128)(2,1)S(1)}, u32[]{:S(2)}, u32[]{:S(2)}) collective-permute-start(bf16[256,128]{1,0:T(8,128)(2,1)S(1)} %get-tuple-element.374), channel_id=1, source_target_pairs={{0,16},{16,32},{32,48},{48,64},{64,80},{80,96},{96,112},{112,128},... | collective-permute-start | bytes 196616 | tf_op jit(solution)/shard_map/while/body/eval_jaxpr/ppermute | solution.py:13
  156.0 8.3 %collective-permute-start.1 = (bf16[256,128]{1,0:T(8,128)(2,1)S(1)}, bf16[256,128]{1,0:T(8,128)(2,1)S(1)}, u32[]{:S(2)}, u32[]{:S(2)}) collective-permute-start(bf16[256,128]{1,0:T(8,128)(2,1)S(1)} %get-tuple-element.375), channel_id=1, source_target_pairs={{0,16},{16,32},{32,48},{48,64},{64,80},{80,96},{96,112},{112,128},... | collective-permute-start | bytes 196616 | tf_op jit(solution)/shard_map/while/body/eval_jaxpr/ppermute | solution.py:13
  164.3 8.3 %collective-permute-start = (bf16[256,128]{1,0:T(8,128)(2,1)S(1)}, bf16[256,128]{1,0:T(8,128)(2,1)S(1)}, u32[]{:S(2)}, u32[]{:S(2)}) collective-permute-start(bf16[256,128]{1,0:T(8,128)(2,1)S(1)} %get-tuple-element.374), channel_id=1, source_target_pairs={{0,16},{16,32},{32,48},{48,64},{64,80},{80,96},{96,112},{112,128},... | collective-permute-start | bytes 196616 | tf_op jit(solution)/shard_map/while/body/eval_jaxpr/ppermute | solution.py:13
  166.3 8.3 %collective-permute-start.1 = (bf16[256,128]{1,0:T(8,128)(2,1)S(1)}, bf16[256,128]{1,0:T(8,128)(2,1)S(1)}, u32[]{:S(2)}, u32[]{:S(2)}) collective-permute-start(bf16[256,128]{1,0:T(8,128)(2,1)S(1)} %get-tuple-element.375), channel_id=1, source_target_pairs={{0,16},{16,32},{32,48},{48,64},{64,80},{80,96},{96,112},{112,128},... | collective-permute-start | bytes 196616 | tf_op jit(solution)/shard_map/while/body/eval_jaxpr/ppermute | solution.py:13
  174.6 8.3 %collective-permute-start = (bf16[256,128]{1,0:T(8,128)(2,1)S(1)}, bf16[256,128]{1,0:T(8,128)(2,1)S(1)}, u32[]{:S(2)}, u32[]{:S(2)}) collective-permute-start(bf16[256,128]{1,0:T(8,128)(2,1)S(1)} %get-tuple-element.374), channel_id=1, source_target_pairs={{0,16},{16,32},{32,48},{48,64},{64,80},{80,96},{96,112},{112,128},... | collective-permute-start | bytes 196616 | tf_op jit(solution)/shard_map/while/body/eval_jaxpr/ppermute | solution.py:13
  176.5 8.3 %collective-permute-start.1 = (bf16[256,128]{1,0:T(8,128)(2,1)S(1)}, bf16[256,128]{1,0:T(8,128)(2,1)S(1)}, u32[]{:S(2)}, u32[]{:S(2)}) collective-permute-start(bf16[256,128]{1,0:T(8,128)(2,1)S(1)} %get-tuple-element.375), channel_id=1, source_target_pairs={{0,16},{16,32},{32,48},{48,64},{64,80},{80,96},{96,112},{112,128},... | collective-permute-start | bytes 196616 | tf_op jit(solution)/shard_map/while/body/eval_jaxpr/ppermute | solution.py:13
  251.5 6.6 %collective-permute-start.11 = (bf16[640,128]{1,0:T(8,128)(2,1)}, bf16[640,128]{1,0:T(8,128)(2,1)}, u32[]{:S(2)}, u32[]{:S(2)}) collective-permute-start(bf16[640,128]{1,0:T(8,128)(2,1)} %collective-permute-done.10), channel_id=1, source_target_pairs={{0,1},{1,2},{2,3},{3,4},{4,5},{5,6},{6,7},{7,8},{8,9},{9,10},{10,1... | collective-permute-start | bytes 491528 | tf_op jit(solution)/shard_map/ppermute | solution.py:109
  252.6 14.8 %all-to-all-start = ((bf16[32,20,128]{2,1,0:T(8,128)(2,1)}), bf16[32,20,128]{2,1,0:T(8,128)(2,1)S(1)}, u32[]{:S(2)}, u32[]{:S(2)}) async-start(bf16[32,20,128]{2,1,0:T(8,128)(2,1)} %all_to_all.24), calls=%async_computation | async-start | bytes 393216 | tf_op jit(solution)/shard_map/all_to_all | solution.py:103
  258.0 65.7 %all-gather.2.cloned.1.call-start = ((), (), s32[]{:S(2)}) async-start(), calls=%async_computation.4 | async-start | bytes 2785280 | tf_op jit(solution)/shard_map/all_gather | solution.py:114
  268.1 131.6 %reduce-scatter.4.cloned.1.call-start = ((), (), s32[]{:S(2)}) async-start(), calls=%async_computation.5 | async-start | bytes 2785280
  283.4 7.7 %collective-permute-start.16 = (bf16[640,128]{1,0:T(8,128)(2,1)S(1)}, bf16[640,128]{1,0:T(8,128)(2,1)S(1)}, u32[]{:S(2)}, u32[]{:S(2)}) collective-permute-start(bf16[640,128]{1,0:T(8,128)(2,1)S(1)} %collective-permute-done.15), channel_id=1, source_target_pairs={{0,1},{1,2},{2,3},{3,4},{4,5},{5,6},{6,7},{7,8},{8,9},{9,10},{10,1... | collective-permute-start | bytes 491528 | tf_op jit(solution)/shard_map/ppermute | solution.py:109
  291.8 6.9 %collective-permute-start.17 = (bf16[640,128]{1,0:T(8,128)(2,1)S(1)}, bf16[640,128]{1,0:T(8,128)(2,1)}, u32[]{:S(2)}, u32[]{:S(2)}) collective-permute-start(bf16[640,128]{1,0:T(8,128)(2,1)S(1)} %collective-permute-done.16), channel_id=1, source_target_pairs={{0,1},{1,2},{2,3},{3,4},{4,5},{5,6},{6,7},{7,8},{8,9},{9,10},{10,1... | collective-permute-start | bytes 491528 | tf_op jit(solution)/shard_map/ppermute | solution.py:109
  298.8 7.0 %collective-permute-start.18 = (bf16[640,128]{1,0:T(8,128)(2,1)}, bf16[640,128]{1,0:T(8,128)(2,1)}, u32[]{:S(2)}, u32[]{:S(2)}) collective-permute-start(bf16[640,128]{1,0:T(8,128)(2,1)} %collective-permute-done.17), channel_id=1, source_target_pairs={{0,1},{1,2},{2,3},{3,4},{4,5},{5,6},{6,7},{7,8},{8,9},{9,10},{10,1... | collective-permute-start | bytes 491528 | tf_op jit(solution)/shard_map/ppermute | solution.py:109
  401.5 19.9 %all-to-all-start.2 = ((bf16[128,32,20]{0,2,1:T(8,128)(2,1)}), bf16[128,32,20]{0,2,1:T(8,128)(2,1)S(1)}, u32[]{:S(2)}, u32[]{:S(2)}) async-start(bf16[128,32,20]{0,2,1:T(8,128)(2,1)} %all_to_all.30), calls=%async_computation.2 | async-start | bytes 393216 | tf_op jit(solution)/shard_map/all_to_all | solution.py:135
  436.7 6.9 %collective-permute-start.2 = (bf16[256,128]{1,0:T(8,128)(2,1)S(1)}, bf16[256,128]{1,0:T(8,128)(2,1)S(1)}, u32[]{:S(2)}, u32[]{:S(2)}) collective-permute-start(bf16[256,128]{1,0:T(8,128)(2,1)S(1)} %get-tuple-element.397), channel_id=1, source_target_pairs={{16,0},{32,16},{48,32},{64,48},{80,64},{96,80},{112,96},{128,112},... | collective-permute-start | bytes 196616 | tf_op jit(solution)/shard_map/while/body/eval_jaxpr/ppermute | solution.py:13
  439.9 6.6 %collective-permute-start.3 = (bf16[256,128]{1,0:T(8,128)(2,1)S(1)}, bf16[256,128]{1,0:T(8,128)(2,1)S(1)}, u32[]{:S(2)}, u32[]{:S(2)}) collective-permute-start(bf16[256,128]{1,0:T(8,128)(2,1)S(1)} %get-tuple-element.398), channel_id=1, source_target_pairs={{16,0},{32,16},{48,32},{64,48},{80,64},{96,80},{112,96},{128,112},... | collective-permute-start | bytes 196616 | tf_op jit(solution)/shard_map/while/body/eval_jaxpr/ppermute | solution.py:13
  447.4 7.3 %collective-permute-start.2 = (bf16[256,128]{1,0:T(8,128)(2,1)S(1)}, bf16[256,128]{1,0:T(8,128)(2,1)S(1)}, u32[]{:S(2)}, u32[]{:S(2)}) collective-permute-start(bf16[256,128]{1,0:T(8,128)(2,1)S(1)} %get-tuple-element.397), channel_id=1, source_target_pairs={{16,0},{32,16},{48,32},{64,48},{80,64},{96,80},{112,96},{128,112},... | collective-permute-start | bytes 196616 | tf_op jit(solution)/shard_map/while/body/eval_jaxpr/ppermute | solution.py:13
  475.5 6.5 %collective-permute-start.3 = (bf16[256,128]{1,0:T(8,128)(2,1)S(1)}, bf16[256,128]{1,0:T(8,128)(2,1)S(1)}, u32[]{:S(2)}, u32[]{:S(2)}) collective-permute-start(bf16[256,128]{1,0:T(8,128)(2,1)S(1)} %get-tuple-element.398), channel_id=1, source_target_pairs={{16,0},{32,16},{48,32},{64,48},{80,64},{96,80},{112,96},{128,112},... | collective-permute-start | bytes 196616 | tf_op jit(solution)/shard_map/while/body/eval_jaxpr/ppermute | solution.py:13
  527.3 6.6 %collective-permute-start.2 = (bf16[256,128]{1,0:T(8,128)(2,1)S(1)}, bf16[256,128]{1,0:T(8,128)(2,1)S(1)}, u32[]{:S(2)}, u32[]{:S(2)}) collective-permute-start(bf16[256,128]{1,0:T(8,128)(2,1)S(1)} %get-tuple-element.397), channel_id=1, source_target_pairs={{16,0},{32,16},{48,32},{64,48},{80,64},{96,80},{112,96},{128,112},... | collective-permute-start | bytes 196616 | tf_op jit(solution)/shard_map/while/body/eval_jaxpr/ppermute | solution.py:13
  542.5 6.4 %collective-permute-start.3 = (bf16[256,128]{1,0:T(8,128)(2,1)S(1)}, bf16[256,128]{1,0:T(8,128)(2,1)S(1)}, u32[]{:S(2)}, u32[]{:S(2)}) collective-permute-start(bf16[256,128]{1,0:T(8,128)(2,1)S(1)} %get-tuple-element.398), channel_id=1, source_target_pairs={{16,0},{32,16},{48,32},{64,48},{80,64},{96,80},{112,96},{128,112},... | collective-permute-start | bytes 196616 | tf_op jit(solution)/shard_map/while/body/eval_jaxpr/ppermute | solution.py:13
  583.2 6.7 %collective-permute-start.2 = (bf16[256,128]{1,0:T(8,128)(2,1)S(1)}, bf16[256,128]{1,0:T(8,128)(2,1)S(1)}, u32[]{:S(2)}, u32[]{:S(2)}) collective-permute-start(bf16[256,128]{1,0:T(8,128)(2,1)S(1)} %get-tuple-element.397), channel_id=1, source_target_pairs={{16,0},{32,16},{48,32},{64,48},{80,64},{96,80},{112,96},{128,112},... | collective-permute-start | bytes 196616 | tf_op jit(solution)/shard_map/while/body/eval_jaxpr/ppermute | solution.py:13
  587.2 6.7 %collective-permute-start.3 = (bf16[256,128]{1,0:T(8,128)(2,1)S(1)}, bf16[256,128]{1,0:T(8,128)(2,1)S(1)}, u32[]{:S(2)}, u32[]{:S(2)}) collective-permute-start(bf16[256,128]{1,0:T(8,128)(2,1)S(1)} %get-tuple-element.398), channel_id=1, source_target_pairs={{16,0},{32,16},{48,32},{64,48},{80,64},{96,80},{112,96},{128,112},... | collective-permute-start | bytes 196616 | tf_op jit(solution)/shard_map/while/body/eval_jaxpr/ppermute | solution.py:13
  (53 other events, 730.8 us)
Sparse Core Ops, SparseCore 0:
  268.2 44.3 all-gather.1
  333.6 66.0 reduce-scatter.3
